TPU v7x, 32 devices: a whole 2x2x4 slice. The times are simulated.
32 devices in a mesh: sub: 8 (over z, y), blk: 4 (over x, core).
Axes of the slice: x: 2, y: 2, z: 4, core: 2. Of those that a mesh axis runs over, the one named last changes fastest.
Arguments:
- initial_state: float32 [8, 64, 2048], P('sub', None, 'blk'), may hold values from -6 to 6
- source: bfloat16 [8, 8, 64, 2048], P('sub', None, None, 'blk'), may hold values from -6 to 6
- inverse_diag: float32 [8, 2048], P('sub', 'blk'), may hold values from 0.5 to 0.85
- inverse_off: bfloat16 [8, 2048, 2048], P('sub', None, 'blk'), may hold values from -0.032958984 to 0.032958984
- coupling: float32 [8, 128], P('sub', 'blk'), may hold values from 0.3 to 3
- initial_waves: bfloat16 [8, 128, 512], P('sub', 'blk'), may hold values from -6 to 6
- bucket: int32 [8], P('sub'), may hold values from 0 to 2
- partner: int32 [8, 128], P('sub', 'blk'), may hold values from 0 to 7
- position_of: int32 [8], replicated, may hold values from 0 to 7, each once
Outputs:
- last_state: float32 [8, 64, 2048], P('sub', None, 'blk')
- waveform: float32 [8, 128, 512], P('sub', 'blk')
Inputs may be any that keep to these rules, and one draw needn't show every extreme that they name: A subcircuit of bucket b takes 8 / 2 ** (2 - b) implicit Euler steps. `position_of`: a permutation.
All inputs are finite; a program needn't handle non-finite values.
Results may differ from a plain program's by a relative error of at most 0.0052.
Values may be sent and summed in bfloat16 or wider, within the bound.
A program may use at most 64 MiB of HBM per device.

v0:
```python
import jax
import jax.numpy as jnp
from jax import lax
from jax.sharding import PartitionSpec as P

SWEEPS = 2


def step_count(bucket, refined_points):
    return jnp.where(
        bucket == 0,
        refined_points // 4,
        jnp.where(bucket == 1, refined_points // 2, refined_points),
    ).astype(jnp.int32)


def port_fetch(waves, selector):
    return jnp.einsum(
        "qjr,rjc->qjc",
        selector,
        lax.all_gather(waves, "sub", axis=0, tiled=True),
        preferred_element_type=jnp.float32,
    ).astype(jnp.bfloat16)


def spread_ports(injected, stride):
    padded = jnp.pad(injected[..., None], [(0, 0)] * injected.ndim + [(0, stride - 1)])
    return padded.reshape(injected.shape[:-1] + (injected.shape[-1] * stride,))


def run_together(
    initial_state, source, inverse_diag, inverse_off, coupling, step_total, spacing, incoming
):
    sub_dev, corners, node_block = initial_state.shape
    refined_points = source.shape[1]
    ports_block = coupling.shape[1]
    stride = node_block // ports_block
    spacing_float = spacing.astype(jnp.float32)
    driven = incoming.astype(jnp.float32).reshape(sub_dev, ports_block, refined_points, corners)
    points = jnp.arange(refined_points, dtype=jnp.int32)

    def contract(totals, shard_rows):
        return totals + jnp.einsum(
            "qcn,qnm->qcm", shard_rows, inverse_off, preferred_element_type=jnp.float32
        )

    def advance(time_step_index, carried):
        current, sample_times = carried
        fine_index = (time_step_index + 1) * spacing - 1
        chosen = points[None, :] == fine_index[:, None]
        forcing = jnp.einsum(
            "qf,qfcn->qcn", chosen.astype(jnp.bfloat16), source, preferred_element_type=jnp.float32
        )
        injected = coupling[:, :, None] * jnp.einsum(
            "qf,qjfc->qjc", chosen.astype(jnp.float32), driven, precision=lax.Precision.HIGHEST
        )
        spread = spread_ports(jnp.swapaxes(injected, 1, 2), stride)
        loop_argument = (current + spacing_float[:, None, None] * (forcing + spread)).astype(
            jnp.bfloat16
        )
        loop_argument = lax.optimization_barrier(loop_argument)
        diagonal_term = inverse_diag[:, None, :] * loop_argument.astype(jnp.float32)
        updated = contract(diagonal_term, lax.all_gather(loop_argument, "blk", axis=2, tiled=True))
        active = time_step_index < step_total
        updated = jnp.where(active[:, None, None], updated, current)
        port_values = updated.reshape(sub_dev, corners, ports_block, stride)[:, :, :, 0]
        sample_times = lax.dynamic_update_index_in_dim(
            sample_times, port_values, time_step_index, 1
        )
        return (updated, sample_times)

    sample_times = jnp.zeros((sub_dev, refined_points, corners, ports_block), jnp.float32)
    last_state, sample_times = lax.fori_loop(
        0, refined_points, advance, (initial_state, sample_times)
    )
    kept_values = (points[None, :, None] // spacing[:, None, None] == points[None, None, :]).astype(
        jnp.float32
    )
    waveform = jnp.einsum(
        "qfk,qkcp->qpfc", kept_values, sample_times, precision=lax.Precision.HIGHEST
    )
    return (last_state, waveform.reshape(sub_dev, ports_block, refined_points * corners))


def shards(
    initial_state,
    source,
    inverse_diag,
    inverse_off,
    coupling,
    initial_waves,
    bucket,
    partner,
    position_of,
):
    refined_points = source.shape[1]
    subs_all = position_of.shape[0]
    identities = jnp.arange(subs_all, dtype=jnp.int32)
    located = jnp.sum(
        jnp.where(partner[:, :, None] == identities[None, None, :], position_of[None, None, :], 0),
        axis=2,
    )
    selector = (located[:, :, None] == identities[None, None, :]).astype(jnp.bfloat16)
    step_total = step_count(bucket, refined_points)
    spacing = refined_points // step_total
    waves = initial_waves
    for sweep_index in range(SWEEPS):
        incoming = port_fetch(waves, selector)
        last_state, waveform = run_together(
            initial_state,
            source,
            inverse_diag,
            inverse_off,
            coupling,
            step_total,
            spacing,
            incoming,
        )
        waves = waveform.astype(jnp.bfloat16)
    return (last_state, waveform)


def solution(mesh):
    return jax.shard_map(
        shards,
        mesh=mesh,
        in_specs=(
            P("sub", None, "blk"),
            P("sub", None, None, "blk"),
            P("sub", "blk"),
            P("sub", None, "blk"),
            P("sub", "blk"),
            P("sub", "blk", None),
            P("sub"),
            P("sub", "blk"),
            P(),
        ),
        out_specs=(P("sub", None, "blk"), P("sub", "blk", None)),
        check_vma=False,
    )
```

profile of v0, /device:TPU:0, one launch (start us, length us, event | category | flops | bytes accessed | tf_op | source)
XLA Modules:
  0.0 216.6 jit_solution(17633719554943924317)
XLA Ops:
  3.0 32.8 %all_gather.26 = bf16[8,32,512]{2,1,0:T(8,128)(2,1)S(1)} all-gather(bf16[1,32,512]{2,1,0:T(8,128)(2,1)} %param.20), channel_id=1, replica_groups=mesh['sub'=8,'blk'=4] {'sub'}, dimensions={0}, use_global_device_ids=true | all-gather | bytes 294912 | tf_op jit(solution)/shard_map/all_gather | solution.py:21
  36.2 73.8 %while.36 = (s32[]{:T(128)}, f32[1,64,512]{2,1,0:T(8,128)S(1)}, f32[1,8,64,32]{2,3,1,0:T(8,128)S(1)}, s32[1]{0:T(128)}, f32[1,512]{1,0:T(1,128)}, /*index=5*/f32...) while((s32[]{:T(128)}, f32[1,64,512]{2,1,0:T(8,128)S(1)}, ...), condition=%wide.region_2.3_spmd.clone, body=%wide.region_1.2_spmd.clone.sunk | while | flops 135202832 | bytes 13330811 | solution.py:73
  37.4 1.4 fusion.101
  38.9 5.8 %all_gather.32 = bf16[1,64,2048]{2,1,0:T(8,128)(2,1)S(1)} all-gather(bf16[1,64,512]{2,1,0:T(8,128)(2,1)S(1)} %fusion.102), channel_id=1, replica_groups=mesh['sub'=8,'blk'=4] {'blk'}, dimensions={2}, use_global_device_ids=true | all-gather | bytes 327680 | tf_op jit(solution)/shard_map/while/body/eval_jaxpr/all_gather | solution.py:63
  46.6 1.4 fusion.101
  48.1 5.9 %all_gather.32 = bf16[1,64,2048]{2,1,0:T(8,128)(2,1)S(1)} all-gather(bf16[1,64,512]{2,1,0:T(8,128)(2,1)S(1)} %fusion.102), channel_id=1, replica_groups=mesh['sub'=8,'blk'=4] {'blk'}, dimensions={2}, use_global_device_ids=true | all-gather | bytes 327680 | tf_op jit(solution)/shard_map/while/body/eval_jaxpr/all_gather | solution.py:63
  55.8 1.4 fusion.101
  57.3 5.9 %all_gather.32 = bf16[1,64,2048]{2,1,0:T(8,128)(2,1)S(1)} all-gather(bf16[1,64,512]{2,1,0:T(8,128)(2,1)S(1)} %fusion.102), channel_id=1, replica_groups=mesh['sub'=8,'blk'=4] {'blk'}, dimensions={2}, use_global_device_ids=true | all-gather | bytes 327680 | tf_op jit(solution)/shard_map/while/body/eval_jaxpr/all_gather | solution.py:63
  65.1 1.4 fusion.101
  66.6 5.9 %all_gather.32 = bf16[1,64,2048]{2,1,0:T(8,128)(2,1)S(1)} all-gather(bf16[1,64,512]{2,1,0:T(8,128)(2,1)S(1)} %fusion.102), channel_id=1, replica_groups=mesh['sub'=8,'blk'=4] {'blk'}, dimensions={2}, use_global_device_ids=true | all-gather | bytes 327680 | tf_op jit(solution)/shard_map/while/body/eval_jaxpr/all_gather | solution.py:63
  75.8 5.9 %all_gather.32 = bf16[1,64,2048]{2,1,0:T(8,128)(2,1)S(1)} all-gather(bf16[1,64,512]{2,1,0:T(8,128)(2,1)S(1)} %fusion.102), channel_id=1, replica_groups=mesh['sub'=8,'blk'=4] {'blk'}, dimensions={2}, use_global_device_ids=true | all-gather | bytes 327680 | tf_op jit(solution)/shard_map/while/body/eval_jaxpr/all_gather | solution.py:63
  83.5 1.4 fusion.101
  85.0 5.9 %all_gather.32 = bf16[1,64,2048]{2,1,0:T(8,128)(2,1)S(1)} all-gather(bf16[1,64,512]{2,1,0:T(8,128)(2,1)S(1)} %fusion.102), channel_id=1, replica_groups=mesh['sub'=8,'blk'=4] {'blk'}, dimensions={2}, use_global_device_ids=true | all-gather | bytes 327680 | tf_op jit(solution)/shard_map/while/body/eval_jaxpr/all_gather | solution.py:63
  92.8 1.4 fusion.101
  94.3 5.9 %all_gather.32 = bf16[1,64,2048]{2,1,0:T(8,128)(2,1)S(1)} all-gather(bf16[1,64,512]{2,1,0:T(8,128)(2,1)S(1)} %fusion.102), channel_id=1, replica_groups=mesh['sub'=8,'blk'=4] {'blk'}, dimensions={2}, use_global_device_ids=true | all-gather | bytes 327680 | tf_op jit(solution)/shard_map/while/body/eval_jaxpr/all_gather | solution.py:63
  103.5 5.9 %all_gather.32 = bf16[1,64,2048]{2,1,0:T(8,128)(2,1)S(1)} all-gather(bf16[1,64,512]{2,1,0:T(8,128)(2,1)S(1)} %fusion.102), channel_id=1, replica_groups=mesh['sub'=8,'blk'=4] {'blk'}, dimensions={2}, use_global_device_ids=true | all-gather | bytes 327680 | tf_op jit(solution)/shard_map/while/body/eval_jaxpr/all_gather | solution.py:63
  110.5 30.8 %all_gather.27 = bf16[8,32,512]{2,1,0:T(8,128)(2,1)S(1)} all-gather(bf16[1,32,512]{2,1,0:T(8,128)(2,1)S(1)} %convert_element_type.111), channel_id=1, replica_groups=mesh['sub'=8,'blk'=4] {'sub'}, dimensions={0}, use_global_device_ids=true | all-gather | bytes 294912 | tf_op jit(solution)/shard_map/all_gather | solution.py:21
  141.7 73.8 %while.37 = (s32[]{:T(128)}, f32[1,64,512]{2,1,0:T(8,128)S(1)}, f32[1,8,64,32]{2,3,1,0:T(8,128)S(1)}, s32[1]{0:T(128)}, f32[1,512]{1,0:T(1,128)}, /*index=5*/f32...) while((s32[]{:T(128)}, f32[1,64,512]{2,1,0:T(8,128)S(1)}, ...), condition=%wide.region_4.6_spmd.clone, body=%wide.region_3.5_spmd.clone.sunk | while | flops 135202832 | bytes 13330811 | solution.py:73
  143.0 1.4 fusion.111
  144.5 5.8 %all_gather.33 = bf16[1,64,2048]{2,1,0:T(8,128)(2,1)S(1)} all-gather(bf16[1,64,512]{2,1,0:T(8,128)(2,1)S(1)} %fusion.112), channel_id=1, replica_groups=mesh['sub'=8,'blk'=4] {'blk'}, dimensions={2}, use_global_device_ids=true | all-gather | bytes 327680 | tf_op jit(solution)/shard_map/while/body/eval_jaxpr/all_gather | solution.py:63
  153.6 5.9 %all_gather.33 = bf16[1,64,2048]{2,1,0:T(8,128)(2,1)S(1)} all-gather(bf16[1,64,512]{2,1,0:T(8,128)(2,1)S(1)} %fusion.112), channel_id=1, replica_groups=mesh['sub'=8,'blk'=4] {'blk'}, dimensions={2}, use_global_device_ids=true | all-gather | bytes 327680 | tf_op jit(solution)/shard_map/while/body/eval_jaxpr/all_gather | solution.py:63
  161.4 1.4 fusion.111
  162.9 5.9 %all_gather.33 = bf16[1,64,2048]{2,1,0:T(8,128)(2,1)S(1)} all-gather(bf16[1,64,512]{2,1,0:T(8,128)(2,1)S(1)} %fusion.112), channel_id=1, replica_groups=mesh['sub'=8,'blk'=4] {'blk'}, dimensions={2}, use_global_device_ids=true | all-gather | bytes 327680 | tf_op jit(solution)/shard_map/while/body/eval_jaxpr/all_gather | solution.py:63
  170.6 1.4 fusion.111
  172.1 5.9 %all_gather.33 = bf16[1,64,2048]{2,1,0:T(8,128)(2,1)S(1)} all-gather(bf16[1,64,512]{2,1,0:T(8,128)(2,1)S(1)} %fusion.112), channel_id=1, replica_groups=mesh['sub'=8,'blk'=4] {'blk'}, dimensions={2}, use_global_device_ids=true | all-gather | bytes 327680 | tf_op jit(solution)/shard_map/while/body/eval_jaxpr/all_gather | solution.py:63
  179.8 1.4 fusion.111
  181.3 5.9 %all_gather.33 = bf16[1,64,2048]{2,1,0:T(8,128)(2,1)S(1)} all-gather(bf16[1,64,512]{2,1,0:T(8,128)(2,1)S(1)} %fusion.112), channel_id=1, replica_groups=mesh['sub'=8,'blk'=4] {'blk'}, dimensions={2}, use_global_device_ids=true | all-gather | bytes 327680 | tf_op jit(solution)/shard_map/while/body/eval_jaxpr/all_gather | solution.py:63
  189.1 1.4 fusion.111
  190.6 5.9 %all_gather.33 = bf16[1,64,2048]{2,1,0:T(8,128)(2,1)S(1)} all-gather(bf16[1,64,512]{2,1,0:T(8,128)(2,1)S(1)} %fusion.112), channel_id=1, replica_groups=mesh['sub'=8,'blk'=4] {'blk'}, dimensions={2}, use_global_device_ids=true | all-gather | bytes 327680 | tf_op jit(solution)/shard_map/while/body/eval_jaxpr/all_gather | solution.py:63
  198.3 1.4 fusion.111
  199.8 5.9 %all_gather.33 = bf16[1,64,2048]{2,1,0:T(8,128)(2,1)S(1)} all-gather(bf16[1,64,512]{2,1,0:T(8,128)(2,1)S(1)} %fusion.112), channel_id=1, replica_groups=mesh['sub'=8,'blk'=4] {'blk'}, dimensions={2}, use_global_device_ids=true | all-gather | bytes 327680 | tf_op jit(solution)/shard_map/while/body/eval_jaxpr/all_gather | solution.py:63
  209.0 5.9 %all_gather.33 = bf16[1,64,2048]{2,1,0:T(8,128)(2,1)S(1)} all-gather(bf16[1,64,512]{2,1,0:T(8,128)(2,1)S(1)} %fusion.112), channel_id=1, replica_groups=mesh['sub'=8,'blk'=4] {'blk'}, dimensions={2}, use_global_device_ids=true | all-gather | bytes 327680 | tf_op jit(solution)/shard_map/while/body/eval_jaxpr/all_gather | solution.py:63
  (231 shorter events, 39.2 us)
Async XLA Ops:
  36.2 8.5 %copy-start = (bf16[1,2048,512]{2,1,0:T(8,128)(2,1)S(1)}, bf16[1,2048,512]{2,1,0:T(8,128)(2,1)}, u32[]{:S(2)}) copy-start(bf16[1,2048,512]{2,1,0:T(8,128)(2,1)} %get-tuple-element.845) | copy-start | bytes 6291460 | tf_op jit(solution)/shard_map/while
  36.2 8.5 %copy-start.3 = (f32[1,512]{1,0:T(1,128)S(1)}, f32[1,512]{1,0:T(1,128)}, u32[]{:S(2)}) copy-start(f32[1,512]{1,0:T(1,128)} %get-tuple-element.839) | copy-start | bytes 6148 | tf_op jit(solution)/shard_map/while
  45.4 8.6 %copy-start = (bf16[1,2048,512]{2,1,0:T(8,128)(2,1)S(1)}, bf16[1,2048,512]{2,1,0:T(8,128)(2,1)}, u32[]{:S(2)}) copy-start(bf16[1,2048,512]{2,1,0:T(8,128)(2,1)} %get-tuple-element.845) | copy-start | bytes 6291460 | tf_op jit(solution)/shard_map/while
  45.4 8.6 %copy-start.3 = (f32[1,512]{1,0:T(1,128)S(1)}, f32[1,512]{1,0:T(1,128)}, u32[]{:S(2)}) copy-start(f32[1,512]{1,0:T(1,128)} %get-tuple-element.839) | copy-start | bytes 6148 | tf_op jit(solution)/shard_map/while
  54.6 8.6 %copy-start = (bf16[1,2048,512]{2,1,0:T(8,128)(2,1)S(1)}, bf16[1,2048,512]{2,1,0:T(8,128)(2,1)}, u32[]{:S(2)}) copy-start(bf16[1,2048,512]{2,1,0:T(8,128)(2,1)} %get-tuple-element.845) | copy-start | bytes 6291460 | tf_op jit(solution)/shard_map/while
  54.6 8.5 %copy-start.3 = (f32[1,512]{1,0:T(1,128)S(1)}, f32[1,512]{1,0:T(1,128)}, u32[]{:S(2)}) copy-start(f32[1,512]{1,0:T(1,128)} %get-tuple-element.839) | copy-start | bytes 6148 | tf_op jit(solution)/shard_map/while
  63.9 8.6 %copy-start = (bf16[1,2048,512]{2,1,0:T(8,128)(2,1)S(1)}, bf16[1,2048,512]{2,1,0:T(8,128)(2,1)}, u32[]{:S(2)}) copy-start(bf16[1,2048,512]{2,1,0:T(8,128)(2,1)} %get-tuple-element.845) | copy-start | bytes 6291460 | tf_op jit(solution)/shard_map/while
  63.9 8.6 %copy-start.3 = (f32[1,512]{1,0:T(1,128)S(1)}, f32[1,512]{1,0:T(1,128)}, u32[]{:S(2)}) copy-start(f32[1,512]{1,0:T(1,128)} %get-tuple-element.839) | copy-start | bytes 6148 | tf_op jit(solution)/shard_map/while
  73.1 8.6 %copy-start = (bf16[1,2048,512]{2,1,0:T(8,128)(2,1)S(1)}, bf16[1,2048,512]{2,1,0:T(8,128)(2,1)}, u32[]{:S(2)}) copy-start(bf16[1,2048,512]{2,1,0:T(8,128)(2,1)} %get-tuple-element.845) | copy-start | bytes 6291460 | tf_op jit(solution)/shard_map/while
  73.1 8.6 %copy-start.3 = (f32[1,512]{1,0:T(1,128)S(1)}, f32[1,512]{1,0:T(1,128)}, u32[]{:S(2)}) copy-start(f32[1,512]{1,0:T(1,128)} %get-tuple-element.839) | copy-start | bytes 6148 | tf_op jit(solution)/shard_map/while
  82.3 8.6 %copy-start = (bf16[1,2048,512]{2,1,0:T(8,128)(2,1)S(1)}, bf16[1,2048,512]{2,1,0:T(8,128)(2,1)}, u32[]{:S(2)}) copy-start(bf16[1,2048,512]{2,1,0:T(8,128)(2,1)} %get-tuple-element.845) | copy-start | bytes 6291460 | tf_op jit(solution)/shard_map/while
  82.3 8.5 %copy-start.3 = (f32[1,512]{1,0:T(1,128)S(1)}, f32[1,512]{1,0:T(1,128)}, u32[]{:S(2)}) copy-start(f32[1,512]{1,0:T(1,128)} %get-tuple-element.839) | copy-start | bytes 6148 | tf_op jit(solution)/shard_map/while
  91.6 8.6 %copy-start = (bf16[1,2048,512]{2,1,0:T(8,128)(2,1)S(1)}, bf16[1,2048,512]{2,1,0:T(8,128)(2,1)}, u32[]{:S(2)}) copy-start(bf16[1,2048,512]{2,1,0:T(8,128)(2,1)} %get-tuple-element.845) | copy-start | bytes 6291460 | tf_op jit(solution)/shard_map/while
  91.6 8.5 %copy-start.3 = (f32[1,512]{1,0:T(1,128)S(1)}, f32[1,512]{1,0:T(1,128)}, u32[]{:S(2)}) copy-start(f32[1,512]{1,0:T(1,128)} %get-tuple-element.839) | copy-start | bytes 6148 | tf_op jit(solution)/shard_map/while
  100.8 8.6 %copy-start = (bf16[1,2048,512]{2,1,0:T(8,128)(2,1)S(1)}, bf16[1,2048,512]{2,1,0:T(8,128)(2,1)}, u32[]{:S(2)}) copy-start(bf16[1,2048,512]{2,1,0:T(8,128)(2,1)} %get-tuple-element.845) | copy-start | bytes 6291460 | tf_op jit(solution)/shard_map/while
  100.8 8.5 %copy-start.3 = (f32[1,512]{1,0:T(1,128)S(1)}, f32[1,512]{1,0:T(1,128)}, u32[]{:S(2)}) copy-start(f32[1,512]{1,0:T(1,128)} %get-tuple-element.839) | copy-start | bytes 6148 | tf_op jit(solution)/shard_map/while
  141.8 8.5 %copy-start.1 = (bf16[1,2048,512]{2,1,0:T(8,128)(2,1)S(1)}, bf16[1,2048,512]{2,1,0:T(8,128)(2,1)}, u32[]{:S(2)}) copy-start(bf16[1,2048,512]{2,1,0:T(8,128)(2,1)} %get-tuple-element.887) | copy-start | bytes 6291460 | tf_op jit(solution)/shard_map/while
  141.8 8.5 %copy-start.4 = (f32[1,512]{1,0:T(1,128)S(1)}, f32[1,512]{1,0:T(1,128)}, u32[]{:S(2)}) copy-start(f32[1,512]{1,0:T(1,128)} %get-tuple-element.881) | copy-start | bytes 6148 | tf_op jit(solution)/shard_map/while
  150.9 8.6 %copy-start.1 = (bf16[1,2048,512]{2,1,0:T(8,128)(2,1)S(1)}, bf16[1,2048,512]{2,1,0:T(8,128)(2,1)}, u32[]{:S(2)}) copy-start(bf16[1,2048,512]{2,1,0:T(8,128)(2,1)} %get-tuple-element.887) | copy-start | bytes 6291460 | tf_op jit(solution)/shard_map/while
  150.9 8.6 %copy-start.4 = (f32[1,512]{1,0:T(1,128)S(1)}, f32[1,512]{1,0:T(1,128)}, u32[]{:S(2)}) copy-start(f32[1,512]{1,0:T(1,128)} %get-tuple-element.881) | copy-start | bytes 6148 | tf_op jit(solution)/shard_map/while
  160.1 8.6 %copy-start.1 = (bf16[1,2048,512]{2,1,0:T(8,128)(2,1)S(1)}, bf16[1,2048,512]{2,1,0:T(8,128)(2,1)}, u32[]{:S(2)}) copy-start(bf16[1,2048,512]{2,1,0:T(8,128)(2,1)} %get-tuple-element.887) | copy-start | bytes 6291460 | tf_op jit(solution)/shard_map/while
  160.2 8.6 %copy-start.4 = (f32[1,512]{1,0:T(1,128)S(1)}, f32[1,512]{1,0:T(1,128)}, u32[]{:S(2)}) copy-start(f32[1,512]{1,0:T(1,128)} %get-tuple-element.881) | copy-start | bytes 6148 | tf_op jit(solution)/shard_map/while
  169.4 8.6 %copy-start.1 = (bf16[1,2048,512]{2,1,0:T(8,128)(2,1)S(1)}, bf16[1,2048,512]{2,1,0:T(8,128)(2,1)}, u32[]{:S(2)}) copy-start(bf16[1,2048,512]{2,1,0:T(8,128)(2,1)} %get-tuple-element.887) | copy-start | bytes 6291460 | tf_op jit(solution)/shard_map/while
  169.4 8.6 %copy-start.4 = (f32[1,512]{1,0:T(1,128)S(1)}, f32[1,512]{1,0:T(1,128)}, u32[]{:S(2)}) copy-start(f32[1,512]{1,0:T(1,128)} %get-tuple-element.881) | copy-start | bytes 6148 | tf_op jit(solution)/shard_map/while
  178.6 8.6 %copy-start.1 = (bf16[1,2048,512]{2,1,0:T(8,128)(2,1)S(1)}, bf16[1,2048,512]{2,1,0:T(8,128)(2,1)}, u32[]{:S(2)}) copy-start(bf16[1,2048,512]{2,1,0:T(8,128)(2,1)} %get-tuple-element.887) | copy-start | bytes 6291460 | tf_op jit(solution)/shard_map/while
  178.6 8.6 %copy-start.4 = (f32[1,512]{1,0:T(1,128)S(1)}, f32[1,512]{1,0:T(1,128)}, u32[]{:S(2)}) copy-start(f32[1,512]{1,0:T(1,128)} %get-tuple-element.881) | copy-start | bytes 6148 | tf_op jit(solution)/shard_map/while
  187.9 8.6 %copy-start.1 = (bf16[1,2048,512]{2,1,0:T(8,128)(2,1)S(1)}, bf16[1,2048,512]{2,1,0:T(8,128)(2,1)}, u32[]{:S(2)}) copy-start(bf16[1,2048,512]{2,1,0:T(8,128)(2,1)} %get-tuple-element.887) | copy-start | bytes 6291460 | tf_op jit(solution)/shard_map/while
  187.9 8.6 %copy-start.4 = (f32[1,512]{1,0:T(1,128)S(1)}, f32[1,512]{1,0:T(1,128)}, u32[]{:S(2)}) copy-start(f32[1,512]{1,0:T(1,128)} %get-tuple-element.881) | copy-start | bytes 6148 | tf_op jit(solution)/shard_map/while
  197.1 8.6 %copy-start.1 = (bf16[1,2048,512]{2,1,0:T(8,128)(2,1)S(1)}, bf16[1,2048,512]{2,1,0:T(8,128)(2,1)}, u32[]{:S(2)}) copy-start(bf16[1,2048,512]{2,1,0:T(8,128)(2,1)} %get-tuple-element.887) | copy-start | bytes 6291460 | tf_op jit(solution)/shard_map/while
  197.1 8.6 %copy-start.4 = (f32[1,512]{1,0:T(1,128)S(1)}, f32[1,512]{1,0:T(1,128)}, u32[]{:S(2)}) copy-start(f32[1,512]{1,0:T(1,128)} %get-tuple-element.881) | copy-start | bytes 6148 | tf_op jit(solution)/shard_map/while
  206.3 8.6 %copy-start.1 = (bf16[1,2048,512]{2,1,0:T(8,128)(2,1)S(1)}, bf16[1,2048,512]{2,1,0:T(8,128)(2,1)}, u32[]{:S(2)}) copy-start(bf16[1,2048,512]{2,1,0:T(8,128)(2,1)} %get-tuple-element.887) | copy-start | bytes 6291460 | tf_op jit(solution)/shard_map/while
  206.3 8.6 %copy-start.4 = (f32[1,512]{1,0:T(1,128)S(1)}, f32[1,512]{1,0:T(1,128)}, u32[]{:S(2)}) copy-start(f32[1,512]{1,0:T(1,128)} %get-tuple-element.881) | copy-start | bytes 6148 | tf_op jit(solution)/shard_map/while
  (1 other events, 1.0 us)
where the time goes:
time: 217 us
  blocking collectives  157 us (72%)
  matrix products  35 us (16%)
  other arithmetic  15 us (7%)
  local copies, waits for them, and re-layouts  6.51 us (3%)
    all_gather x16, blocking collectives, advance(): lax.all_gather(loop_argument, 'blk', axis=2, tiled=True)  93.5 us
    all_gather x2, blocking collectives, port_fetch(): lax.all_gather(waves, 'sub', axis=0, tiled=True)  63.5 us
    dot_general x16, matrix products, advance(): jnp.einsum('qf,qfcn->qcn', chosen.astype(jnp.bfloat16), source, preferred...  23.2 us
    mul x16, other arithmetic, advance(): coupling[:, :, None]  13.5 us
    dot_general x16, matrix products, contract(): jnp.einsum('qcn,qnm->qcm', shard_rows, inverse_off, preferred_element_typ...  7.7 us

commit v1 on v0

--- a/solution.py
+++ b/solution.py
@@ -4,6 +4,18 @@
 from jax.sharding import PartitionSpec as P
 
 SWEEPS = 2
+
+
+def ring_product(x, axis, dim, term):
+    count, mine = (lax.axis_size(axis), lax.axis_index(axis))
+    backward = [(i, (i - 1) % count) for i in range(count)]
+    span = x.shape[dim]
+    carried = x
+    total = term(carried, mine * span)
+    for step in range(1, count):
+        carried = lax.ppermute(carried, axis, backward)
+        total = total + term(carried, (mine + step) % count * span)
+    return total
 
 
 def step_count(bucket, refined_points):
@@ -15,11 +27,16 @@
 
 
 def port_fetch(waves, selector):
-    return jnp.einsum(
-        "qjr,rjc->qjc",
-        selector,
-        lax.all_gather(waves, "sub", axis=0, tiled=True),
-        preferred_element_type=jnp.float32,
+    return ring_product(
+        waves,
+        "sub",
+        0,
+        lambda own_block, at: jnp.einsum(
+            "qjr,rjc->qjc",
+            lax.dynamic_slice_in_dim(selector, at, own_block.shape[0], axis=2),
+            own_block,
+            preferred_element_type=jnp.float32,
+        ),
     ).astype(jnp.bfloat16)
 
 

time: 217 us -> 247 us (1.14)
  starting transfers between devices: 0 us -> 71.3 us
  blocking collectives: 157 us -> 93.5 us
  waiting for transfers between devices: 0 us -> 21 us
    ppermute x0 -> x14, starting transfers between devices: none -> 71.3 us  [ring_product(): carried = lax.ppermute(carried, axis, backward)]
    all_gather x2 -> x0, blocking collectives: 63.5 us -> none  [port_fetch(): lax.all_gather(waves, 'sub', axis=0, tiled=True)]
    ppermute x0 -> x14, waiting for transfers between devices: none -> 21 us  [ring_product(): carried = lax.ppermute(carried, axis, backward)]
  transfers between devices with their start and end apart: 0 -> 14, of which waited for: 0 -> 14; matrix products, arithmetic and copies ran while one was open for 0% -> 0% of each run, Pallas kernels for 0% -> 0%
where the time goes in v1:
time: 247 us; the launch traced here: 246 us
  blocking collectives  93.5 us (38%)
  starting transfers between devices  71.3 us (29%)
  matrix products  34.5 us (14%)
  waiting for transfers between devices  21 us (9%)
  other arithmetic  15.9 us (6%)
  local copies, waits for them, and re-layouts  6.61 us (3%)
    all_gather x16, blocking collectives, advance(): lax.all_gather(loop_argument, 'blk', axis=2, tiled=True)  93.5 us
    ppermute x14, starting transfers between devices, ring_product(): carried = lax.ppermute(carried, axis, backward)  71.3 us
    dot_general x16, matrix products, advance(): jnp.einsum('qf,qfcn->qcn', chosen.astype(jnp.bfloat16), source, preferred...  23.2 us
    ppermute x14, waiting for transfers between devices, ring_product(): carried = lax.ppermute(carried, axis, backward)  21 us
    mul x16, other arithmetic, advance(): coupling[:, :, None]  13.5 us
    dot_general x16, matrix products, contract(): jnp.einsum('qcn,qnm->qcm', shard_rows, inverse_off, preferred_element_typ...  7.7 us
  transfers between devices with their start and end apart: 14, of which 14 were waited for; matrix products, arithmetic and copies ran while one was open for 0% of the time, Pallas kernels for 0%

profile of v1, /device:TPU:0, one launch (start us, length us, event | category | flops | bytes accessed | tf_op | source)
XLA Modules:
  0.0 245.8 jit_solution(10093438271665496197)
XLA Ops:
  1.5 6.0 %collective-permute-start = (bf16[1,32,512]{2,1,0:T(8,128)(2,1)}, bf16[1,32,512]{2,1,0:T(8,128)(2,1)S(1)}, u32[]{:S(2)}, u32[]{:S(2)}) collective-permute-start(bf16[1,32,512]{2,1,0:T(8,128)(2,1)} %param.20), channel_id=1, source_target_pairs={{0,28},{4,0},{8,4},{12,8},{16,12},{20,16},{24,20},{28,24},{1,29},{... | collective-permute-start | bytes 98312 | tf_op jit(solution)/shard_map/ppermute | solution.py:16
  9.5 4.9 %collective-permute-start.1 = (bf16[1,32,512]{2,1,0:T(8,128)(2,1)S(1)}, bf16[1,32,512]{2,1,0:T(8,128)(2,1)S(1)}, u32[]{:S(2)}, u32[]{:S(2)}) collective-permute-start(bf16[1,32,512]{2,1,0:T(8,128)(2,1)S(1)} %collective-permute-done), channel_id=1, source_target_pairs={{0,28},{4,0},{8,4},{12,8},{16,12},{20,16},{24,20},{28,24},{1,29},{... | collective-permute-start | bytes 98312 | tf_op jit(solution)/shard_map/ppermute | solution.py:16
  16.0 5.0 %collective-permute-start.2 = (bf16[1,32,512]{2,1,0:T(8,128)(2,1)S(1)}, bf16[1,32,512]{2,1,0:T(8,128)(2,1)S(1)}, u32[]{:S(2)}, u32[]{:S(2)}) collective-permute-start(bf16[1,32,512]{2,1,0:T(8,128)(2,1)S(1)} %collective-permute-done.1), channel_id=1, source_target_pairs={{0,28},{4,0},{8,4},{12,8},{16,12},{20,16},{24,20},{28,24},{1,29},{... | collective-permute-start | bytes 98312 | tf_op jit(solution)/shard_map/ppermute | solution.py:16
  22.6 5.0 %collective-permute-start.3 = (bf16[1,32,512]{2,1,0:T(8,128)(2,1)S(1)}, bf16[1,32,512]{2,1,0:T(8,128)(2,1)S(1)}, u32[]{:S(2)}, u32[]{:S(2)}) collective-permute-start(bf16[1,32,512]{2,1,0:T(8,128)(2,1)S(1)} %collective-permute-done.2), channel_id=1, source_target_pairs={{0,28},{4,0},{8,4},{12,8},{16,12},{20,16},{24,20},{28,24},{1,29},{... | collective-permute-start | bytes 98312 | tf_op jit(solution)/shard_map/ppermute | solution.py:16
  29.2 5.0 %collective-permute-start.4 = (bf16[1,32,512]{2,1,0:T(8,128)(2,1)S(1)}, bf16[1,32,512]{2,1,0:T(8,128)(2,1)S(1)}, u32[]{:S(2)}, u32[]{:S(2)}) collective-permute-start(bf16[1,32,512]{2,1,0:T(8,128)(2,1)S(1)} %collective-permute-done.3), channel_id=1, source_target_pairs={{0,28},{4,0},{8,4},{12,8},{16,12},{20,16},{24,20},{28,24},{1,29},{... | collective-permute-start | bytes 98312 | tf_op jit(solution)/shard_map/ppermute | solution.py:16
  35.8 5.1 %collective-permute-start.5 = (bf16[1,32,512]{2,1,0:T(8,128)(2,1)S(1)}, bf16[1,32,512]{2,1,0:T(8,128)(2,1)S(1)}, u32[]{:S(2)}, u32[]{:S(2)}) collective-permute-start(bf16[1,32,512]{2,1,0:T(8,128)(2,1)S(1)} %collective-permute-done.4), channel_id=1, source_target_pairs={{0,28},{4,0},{8,4},{12,8},{16,12},{20,16},{24,20},{28,24},{1,29},{... | collective-permute-start | bytes 98312 | tf_op jit(solution)/shard_map/ppermute | solution.py:16
  42.5 5.0 %collective-permute-start.6 = (bf16[1,32,512]{2,1,0:T(8,128)(2,1)S(1)}, bf16[1,32,512]{2,1,0:T(8,128)(2,1)S(1)}, u32[]{:S(2)}, u32[]{:S(2)}) collective-permute-start(bf16[1,32,512]{2,1,0:T(8,128)(2,1)S(1)} %collective-permute-done.5), channel_id=1, source_target_pairs={{0,28},{4,0},{8,4},{12,8},{16,12},{20,16},{24,20},{28,24},{1,29},{... | collective-permute-start | bytes 98312 | tf_op jit(solution)/shard_map/ppermute | solution.py:16
  50.1 73.8 %while.36 = (s32[]{:T(128)}, f32[1,64,512]{2,1,0:T(8,128)S(1)}, f32[1,8,64,32]{2,3,1,0:T(8,128)S(1)}, s32[1]{0:T(128)}, f32[1,512]{1,0:T(1,128)}, /*index=5*/f32...) while((s32[]{:T(128)}, f32[1,64,512]{2,1,0:T(8,128)S(1)}, ...), condition=%wide.region_2.3_spmd.clone, body=%wide.region_1.2_spmd.clone.sunk | while | flops 135202832 | bytes 13330811 | solution.py:90
  52.8 5.8 %all_gather.24 = bf16[1,64,2048]{2,1,0:T(8,128)(2,1)S(1)} all-gather(bf16[1,64,512]{2,1,0:T(8,128)(2,1)S(1)} %fusion.127), channel_id=1, replica_groups=mesh['sub'=8,'blk'=4] {'blk'}, dimensions={2}, use_global_device_ids=true | all-gather | bytes 327680 | tf_op jit(solution)/shard_map/while/body/eval_jaxpr/all_gather | solution.py:80
  62.0 5.9 %all_gather.24 = bf16[1,64,2048]{2,1,0:T(8,128)(2,1)S(1)} all-gather(bf16[1,64,512]{2,1,0:T(8,128)(2,1)S(1)} %fusion.127), channel_id=1, replica_groups=mesh['sub'=8,'blk'=4] {'blk'}, dimensions={2}, use_global_device_ids=true | all-gather | bytes 327680 | tf_op jit(solution)/shard_map/while/body/eval_jaxpr/all_gather | solution.py:80
  71.2 5.9 %all_gather.24 = bf16[1,64,2048]{2,1,0:T(8,128)(2,1)S(1)} all-gather(bf16[1,64,512]{2,1,0:T(8,128)(2,1)S(1)} %fusion.127), channel_id=1, replica_groups=mesh['sub'=8,'blk'=4] {'blk'}, dimensions={2}, use_global_device_ids=true | all-gather | bytes 327680 | tf_op jit(solution)/shard_map/while/body/eval_jaxpr/all_gather | solution.py:80
  80.5 5.9 %all_gather.24 = bf16[1,64,2048]{2,1,0:T(8,128)(2,1)S(1)} all-gather(bf16[1,64,512]{2,1,0:T(8,128)(2,1)S(1)} %fusion.127), channel_id=1, replica_groups=mesh['sub'=8,'blk'=4] {'blk'}, dimensions={2}, use_global_device_ids=true | all-gather | bytes 327680 | tf_op jit(solution)/shard_map/while/body/eval_jaxpr/all_gather | solution.py:80
  89.7 5.9 %all_gather.24 = bf16[1,64,2048]{2,1,0:T(8,128)(2,1)S(1)} all-gather(bf16[1,64,512]{2,1,0:T(8,128)(2,1)S(1)} %fusion.127), channel_id=1, replica_groups=mesh['sub'=8,'blk'=4] {'blk'}, dimensions={2}, use_global_device_ids=true | all-gather | bytes 327680 | tf_op jit(solution)/shard_map/while/body/eval_jaxpr/all_gather | solution.py:80
  98.9 5.9 %all_gather.24 = bf16[1,64,2048]{2,1,0:T(8,128)(2,1)S(1)} all-gather(bf16[1,64,512]{2,1,0:T(8,128)(2,1)S(1)} %fusion.127), channel_id=1, replica_groups=mesh['sub'=8,'blk'=4] {'blk'}, dimensions={2}, use_global_device_ids=true | all-gather | bytes 327680 | tf_op jit(solution)/shard_map/while/body/eval_jaxpr/all_gather | solution.py:80
  108.2 5.9 %all_gather.24 = bf16[1,64,2048]{2,1,0:T(8,128)(2,1)S(1)} all-gather(bf16[1,64,512]{2,1,0:T(8,128)(2,1)S(1)} %fusion.127), channel_id=1, replica_groups=mesh['sub'=8,'blk'=4] {'blk'}, dimensions={2}, use_global_device_ids=true | all-gather | bytes 327680 | tf_op jit(solution)/shard_map/while/body/eval_jaxpr/all_gather | solution.py:80
  117.4 5.9 %all_gather.24 = bf16[1,64,2048]{2,1,0:T(8,128)(2,1)S(1)} all-gather(bf16[1,64,512]{2,1,0:T(8,128)(2,1)S(1)} %fusion.127), channel_id=1, replica_groups=mesh['sub'=8,'blk'=4] {'blk'}, dimensions={2}, use_global_device_ids=true | all-gather | bytes 327680 | tf_op jit(solution)/shard_map/while/body/eval_jaxpr/all_gather | solution.py:80
  124.3 5.1 %collective-permute-start.7 = (bf16[1,32,512]{2,1,0:T(8,128)(2,1)S(1)}, bf16[1,32,512]{2,1,0:T(8,128)(2,1)S(1)}, u32[]{:S(2)}, u32[]{:S(2)}) collective-permute-start(bf16[1,32,512]{2,1,0:T(8,128)(2,1)S(1)} %convert_element_type.109), channel_id=1, source_target_pairs={{0,28},{4,0},{8,4},{12,8},{16,12},{20,16},{24,20},{28,24},{1,29},{... | collective-permute-start | bytes 98312 | tf_op jit(solution)/shard_map/ppermute | solution.py:16
  131.0 5.0 %collective-permute-start.8 = (bf16[1,32,512]{2,1,0:T(8,128)(2,1)S(1)}, bf16[1,32,512]{2,1,0:T(8,128)(2,1)S(1)}, u32[]{:S(2)}, u32[]{:S(2)}) collective-permute-start(bf16[1,32,512]{2,1,0:T(8,128)(2,1)S(1)} %collective-permute-done.7), channel_id=1, source_target_pairs={{0,28},{4,0},{8,4},{12,8},{16,12},{20,16},{24,20},{28,24},{1,29},{... | collective-permute-start | bytes 98312 | tf_op jit(solution)/shard_map/ppermute | solution.py:16
  137.6 5.0 %collective-permute-start.9 = (bf16[1,32,512]{2,1,0:T(8,128)(2,1)S(1)}, bf16[1,32,512]{2,1,0:T(8,128)(2,1)S(1)}, u32[]{:S(2)}, u32[]{:S(2)}) collective-permute-start(bf16[1,32,512]{2,1,0:T(8,128)(2,1)S(1)} %collective-permute-done.8), channel_id=1, source_target_pairs={{0,28},{4,0},{8,4},{12,8},{16,12},{20,16},{24,20},{28,24},{1,29},{... | collective-permute-start | bytes 98312 | tf_op jit(solution)/shard_map/ppermute | solution.py:16
  144.2 5.0 %collective-permute-start.10 = (bf16[1,32,512]{2,1,0:T(8,128)(2,1)S(1)}, bf16[1,32,512]{2,1,0:T(8,128)(2,1)S(1)}, u32[]{:S(2)}, u32[]{:S(2)}) collective-permute-start(bf16[1,32,512]{2,1,0:T(8,128)(2,1)S(1)} %collective-permute-done.9), channel_id=1, source_target_pairs={{0,28},{4,0},{8,4},{12,8},{16,12},{20,16},{24,20},{28,24},{1,29},{... | collective-permute-start | bytes 98312 | tf_op jit(solution)/shard_map/ppermute | solution.py:16
  150.8 5.0 %collective-permute-start.11 = (bf16[1,32,512]{2,1,0:T(8,128)(2,1)S(1)}, bf16[1,32,512]{2,1,0:T(8,128)(2,1)S(1)}, u32[]{:S(2)}, u32[]{:S(2)}) collective-permute-start(bf16[1,32,512]{2,1,0:T(8,128)(2,1)S(1)} %collective-permute-done.10), channel_id=1, source_target_pairs={{0,28},{4,0},{8,4},{12,8},{16,12},{20,16},{24,20},{28,24},{1,29},{... | collective-permute-start | bytes 98312 | tf_op jit(solution)/shard_map/ppermute | solution.py:16
  157.4 5.1 %collective-permute-start.12 = (bf16[1,32,512]{2,1,0:T(8,128)(2,1)S(1)}, bf16[1,32,512]{2,1,0:T(8,128)(2,1)S(1)}, u32[]{:S(2)}, u32[]{:S(2)}) collective-permute-start(bf16[1,32,512]{2,1,0:T(8,128)(2,1)S(1)} %collective-permute-done.11), channel_id=1, source_target_pairs={{0,28},{4,0},{8,4},{12,8},{16,12},{20,16},{24,20},{28,24},{1,29},{... | collective-permute-start | bytes 98312 | tf_op jit(solution)/shard_map/ppermute | solution.py:16
  164.2 5.0 %collective-permute-start.13 = (bf16[1,32,512]{2,1,0:T(8,128)(2,1)S(1)}, bf16[1,32,512]{2,1,0:T(8,128)(2,1)S(1)}, u32[]{:S(2)}, u32[]{:S(2)}) collective-permute-start(bf16[1,32,512]{2,1,0:T(8,128)(2,1)S(1)} %collective-permute-done.12), channel_id=1, source_target_pairs={{0,28},{4,0},{8,4},{12,8},{16,12},{20,16},{24,20},{28,24},{1,29},{... | collective-permute-start | bytes 98312 | tf_op jit(solution)/shard_map/ppermute | solution.py:16
  171.0 73.8 %while.37 = (s32[]{:T(128)}, f32[1,64,512]{2,1,0:T(8,128)S(1)}, f32[1,8,64,32]{2,3,1,0:T(8,128)S(1)}, s32[1]{0:T(128)}, f32[1,512]{1,0:T(1,128)}, /*index=5*/f32...) while((s32[]{:T(128)}, f32[1,64,512]{2,1,0:T(8,128)S(1)}, ...), condition=%wide.region_4.6_spmd.clone, body=%wide.region_3.5_spmd.clone.sunk | while | flops 135202832 | bytes 13330811 | solution.py:90
  173.7 5.8 %all_gather.25 = bf16[1,64,2048]{2,1,0:T(8,128)(2,1)S(1)} all-gather(bf16[1,64,512]{2,1,0:T(8,128)(2,1)S(1)} %fusion.137), channel_id=1, replica_groups=mesh['sub'=8,'blk'=4] {'blk'}, dimensions={2}, use_global_device_ids=true | all-gather | bytes 327680 | tf_op jit(solution)/shard_map/while/body/eval_jaxpr/all_gather | solution.py:80
  182.9 5.9 %all_gather.25 = bf16[1,64,2048]{2,1,0:T(8,128)(2,1)S(1)} all-gather(bf16[1,64,512]{2,1,0:T(8,128)(2,1)S(1)} %fusion.137), channel_id=1, replica_groups=mesh['sub'=8,'blk'=4] {'blk'}, dimensions={2}, use_global_device_ids=true | all-gather | bytes 327680 | tf_op jit(solution)/shard_map/while/body/eval_jaxpr/all_gather | solution.py:80
  192.1 5.9 %all_gather.25 = bf16[1,64,2048]{2,1,0:T(8,128)(2,1)S(1)} all-gather(bf16[1,64,512]{2,1,0:T(8,128)(2,1)S(1)} %fusion.137), channel_id=1, replica_groups=mesh['sub'=8,'blk'=4] {'blk'}, dimensions={2}, use_global_device_ids=true | all-gather | bytes 327680 | tf_op jit(solution)/shard_map/while/body/eval_jaxpr/all_gather | solution.py:80
  201.3 5.9 %all_gather.25 = bf16[1,64,2048]{2,1,0:T(8,128)(2,1)S(1)} all-gather(bf16[1,64,512]{2,1,0:T(8,128)(2,1)S(1)} %fusion.137), channel_id=1, replica_groups=mesh['sub'=8,'blk'=4] {'blk'}, dimensions={2}, use_global_device_ids=true | all-gather | bytes 327680 | tf_op jit(solution)/shard_map/while/body/eval_jaxpr/all_gather | solution.py:80
  210.6 5.9 %all_gather.25 = bf16[1,64,2048]{2,1,0:T(8,128)(2,1)S(1)} all-gather(bf16[1,64,512]{2,1,0:T(8,128)(2,1)S(1)} %fusion.137), channel_id=1, replica_groups=mesh['sub'=8,'blk'=4] {'blk'}, dimensions={2}, use_global_device_ids=true | all-gather | bytes 327680 | tf_op jit(solution)/shard_map/while/body/eval_jaxpr/all_gather | solution.py:80
  219.8 5.9 %all_gather.25 = bf16[1,64,2048]{2,1,0:T(8,128)(2,1)S(1)} all-gather(bf16[1,64,512]{2,1,0:T(8,128)(2,1)S(1)} %fusion.137), channel_id=1, replica_groups=mesh['sub'=8,'blk'=4] {'blk'}, dimensions={2}, use_global_device_ids=true | all-gather | bytes 327680 | tf_op jit(solution)/shard_map/while/body/eval_jaxpr/all_gather | solution.py:80
  229.0 5.9 %all_gather.25 = bf16[1,64,2048]{2,1,0:T(8,128)(2,1)S(1)} all-gather(bf16[1,64,512]{2,1,0:T(8,128)(2,1)S(1)} %fusion.137), channel_id=1, replica_groups=mesh['sub'=8,'blk'=4] {'blk'}, dimensions={2}, use_global_device_ids=true | all-gather | bytes 327680 | tf_op jit(solution)/shard_map/while/body/eval_jaxpr/all_gather | solution.py:80
  238.3 5.9 %all_gather.25 = bf16[1,64,2048]{2,1,0:T(8,128)(2,1)S(1)} all-gather(bf16[1,64,512]{2,1,0:T(8,128)(2,1)S(1)} %fusion.137), channel_id=1, replica_groups=mesh['sub'=8,'blk'=4] {'blk'}, dimensions={2}, use_global_device_ids=true | all-gather | bytes 327680 | tf_op jit(solution)/shard_map/while/body/eval_jaxpr/all_gather | solution.py:80
  (257 shorter events, 78.0 us)
Async XLA Ops:
  1.5 7.9 %collective-permute-start = (bf16[1,32,512]{2,1,0:T(8,128)(2,1)}, bf16[1,32,512]{2,1,0:T(8,128)(2,1)S(1)}, u32[]{:S(2)}, u32[]{:S(2)}) collective-permute-start(bf16[1,32,512]{2,1,0:T(8,128)(2,1)} %param.20), channel_id=1, source_target_pairs={{0,28},{4,0},{8,4},{12,8},{16,12},{20,16},{24,20},{28,24},{1,29},{... | collective-permute-start | bytes 98312 | tf_op jit(solution)/shard_map/ppermute | solution.py:16
  9.5 6.5 %collective-permute-start.1 = (bf16[1,32,512]{2,1,0:T(8,128)(2,1)S(1)}, bf16[1,32,512]{2,1,0:T(8,128)(2,1)S(1)}, u32[]{:S(2)}, u32[]{:S(2)}) collective-permute-start(bf16[1,32,512]{2,1,0:T(8,128)(2,1)S(1)} %collective-permute-done), channel_id=1, source_target_pairs={{0,28},{4,0},{8,4},{12,8},{16,12},{20,16},{24,20},{28,24},{1,29},{... | collective-permute-start | bytes 98312 | tf_op jit(solution)/shard_map/ppermute | solution.py:16
  16.0 6.6 %collective-permute-start.2 = (bf16[1,32,512]{2,1,0:T(8,128)(2,1)S(1)}, bf16[1,32,512]{2,1,0:T(8,128)(2,1)S(1)}, u32[]{:S(2)}, u32[]{:S(2)}) collective-permute-start(bf16[1,32,512]{2,1,0:T(8,128)(2,1)S(1)} %collective-permute-done.1), channel_id=1, source_target_pairs={{0,28},{4,0},{8,4},{12,8},{16,12},{20,16},{24,20},{28,24},{1,29},{... | collective-permute-start | bytes 98312 | tf_op jit(solution)/shard_map/ppermute | solution.py:16
  22.6 6.6 %collective-permute-start.3 = (bf16[1,32,512]{2,1,0:T(8,128)(2,1)S(1)}, bf16[1,32,512]{2,1,0:T(8,128)(2,1)S(1)}, u32[]{:S(2)}, u32[]{:S(2)}) collective-permute-start(bf16[1,32,512]{2,1,0:T(8,128)(2,1)S(1)} %collective-permute-done.2), channel_id=1, source_target_pairs={{0,28},{4,0},{8,4},{12,8},{16,12},{20,16},{24,20},{28,24},{1,29},{... | collective-permute-start | bytes 98312 | tf_op jit(solution)/shard_map/ppermute | solution.py:16
  29.2 6.6 %collective-permute-start.4 = (bf16[1,32,512]{2,1,0:T(8,128)(2,1)S(1)}, bf16[1,32,512]{2,1,0:T(8,128)(2,1)S(1)}, u32[]{:S(2)}, u32[]{:S(2)}) collective-permute-start(bf16[1,32,512]{2,1,0:T(8,128)(2,1)S(1)} %collective-permute-done.3), channel_id=1, source_target_pairs={{0,28},{4,0},{8,4},{12,8},{16,12},{20,16},{24,20},{28,24},{1,29},{... | collective-permute-start | bytes 98312 | tf_op jit(solution)/shard_map/ppermute | solution.py:16
  35.8 6.7 %collective-permute-start.5 = (bf16[1,32,512]{2,1,0:T(8,128)(2,1)S(1)}, bf16[1,32,512]{2,1,0:T(8,128)(2,1)S(1)}, u32[]{:S(2)}, u32[]{:S(2)}) collective-permute-start(bf16[1,32,512]{2,1,0:T(8,128)(2,1)S(1)} %collective-permute-done.4), channel_id=1, source_target_pairs={{0,28},{4,0},{8,4},{12,8},{16,12},{20,16},{24,20},{28,24},{1,29},{... | collective-permute-start | bytes 98312 | tf_op jit(solution)/shard_map/ppermute | solution.py:16
  42.5 6.6 %collective-permute-start.6 = (bf16[1,32,512]{2,1,0:T(8,128)(2,1)S(1)}, bf16[1,32,512]{2,1,0:T(8,128)(2,1)S(1)}, u32[]{:S(2)}, u32[]{:S(2)}) collective-permute-start(bf16[1,32,512]{2,1,0:T(8,128)(2,1)S(1)} %collective-permute-done.5), channel_id=1, source_target_pairs={{0,28},{4,0},{8,4},{12,8},{16,12},{20,16},{24,20},{28,24},{1,29},{... | collective-permute-start | bytes 98312 | tf_op jit(solution)/shard_map/ppermute | solution.py:16
  59.3 8.6 %copy-start = (bf16[1,2048,512]{2,1,0:T(8,128)(2,1)S(1)}, bf16[1,2048,512]{2,1,0:T(8,128)(2,1)}, u32[]{:S(2)}) copy-start(bf16[1,2048,512]{2,1,0:T(8,128)(2,1)} %get-tuple-element.853) | copy-start | bytes 6291460 | tf_op jit(solution)/shard_map/while
  68.5 8.6 %copy-start = (bf16[1,2048,512]{2,1,0:T(8,128)(2,1)S(1)}, bf16[1,2048,512]{2,1,0:T(8,128)(2,1)}, u32[]{:S(2)}) copy-start(bf16[1,2048,512]{2,1,0:T(8,128)(2,1)} %get-tuple-element.853) | copy-start | bytes 6291460 | tf_op jit(solution)/shard_map/while
  68.5 8.6 %copy-start.3 = (f32[1,512]{1,0:T(1,128)S(1)}, f32[1,512]{1,0:T(1,128)}, u32[]{:S(2)}) copy-start(f32[1,512]{1,0:T(1,128)} %get-tuple-element.847) | copy-start | bytes 6148 | tf_op jit(solution)/shard_map/while
  77.8 8.6 %copy-start = (bf16[1,2048,512]{2,1,0:T(8,128)(2,1)S(1)}, bf16[1,2048,512]{2,1,0:T(8,128)(2,1)}, u32[]{:S(2)}) copy-start(bf16[1,2048,512]{2,1,0:T(8,128)(2,1)} %get-tuple-element.853) | copy-start | bytes 6291460 | tf_op jit(solution)/shard_map/while
  77.8 8.6 %copy-start.3 = (f32[1,512]{1,0:T(1,128)S(1)}, f32[1,512]{1,0:T(1,128)}, u32[]{:S(2)}) copy-start(f32[1,512]{1,0:T(1,128)} %get-tuple-element.847) | copy-start | bytes 6148 | tf_op jit(solution)/shard_map/while
  87.0 8.6 %copy-start = (bf16[1,2048,512]{2,1,0:T(8,128)(2,1)S(1)}, bf16[1,2048,512]{2,1,0:T(8,128)(2,1)}, u32[]{:S(2)}) copy-start(bf16[1,2048,512]{2,1,0:T(8,128)(2,1)} %get-tuple-element.853) | copy-start | bytes 6291460 | tf_op jit(solution)/shard_map/while
  96.2 8.6 %copy-start = (bf16[1,2048,512]{2,1,0:T(8,128)(2,1)S(1)}, bf16[1,2048,512]{2,1,0:T(8,128)(2,1)}, u32[]{:S(2)}) copy-start(bf16[1,2048,512]{2,1,0:T(8,128)(2,1)} %get-tuple-element.853) | copy-start | bytes 6291460 | tf_op jit(solution)/shard_map/while
  105.5 8.6 %copy-start = (bf16[1,2048,512]{2,1,0:T(8,128)(2,1)S(1)}, bf16[1,2048,512]{2,1,0:T(8,128)(2,1)}, u32[]{:S(2)}) copy-start(bf16[1,2048,512]{2,1,0:T(8,128)(2,1)} %get-tuple-element.853) | copy-start | bytes 6291460 | tf_op jit(solution)/shard_map/while
  105.5 8.6 %copy-start.3 = (f32[1,512]{1,0:T(1,128)S(1)}, f32[1,512]{1,0:T(1,128)}, u32[]{:S(2)}) copy-start(f32[1,512]{1,0:T(1,128)} %get-tuple-element.847) | copy-start | bytes 6148 | tf_op jit(solution)/shard_map/while
  114.7 8.6 %copy-start = (bf16[1,2048,512]{2,1,0:T(8,128)(2,1)S(1)}, bf16[1,2048,512]{2,1,0:T(8,128)(2,1)}, u32[]{:S(2)}) copy-start(bf16[1,2048,512]{2,1,0:T(8,128)(2,1)} %get-tuple-element.853) | copy-start | bytes 6291460 | tf_op jit(solution)/shard_map/while
  114.7 8.6 %copy-start.3 = (f32[1,512]{1,0:T(1,128)S(1)}, f32[1,512]{1,0:T(1,128)}, u32[]{:S(2)}) copy-start(f32[1,512]{1,0:T(1,128)} %get-tuple-element.847) | copy-start | bytes 6148 | tf_op jit(solution)/shard_map/while
  124.3 6.7 %collective-permute-start.7 = (bf16[1,32,512]{2,1,0:T(8,128)(2,1)S(1)}, bf16[1,32,512]{2,1,0:T(8,128)(2,1)S(1)}, u32[]{:S(2)}, u32[]{:S(2)}) collective-permute-start(bf16[1,32,512]{2,1,0:T(8,128)(2,1)S(1)} %convert_element_type.109), channel_id=1, source_target_pairs={{0,28},{4,0},{8,4},{12,8},{16,12},{20,16},{24,20},{28,24},{1,29},{... | collective-permute-start | bytes 98312 | tf_op jit(solution)/shard_map/ppermute | solution.py:16
  131.0 6.6 %collective-permute-start.8 = (bf16[1,32,512]{2,1,0:T(8,128)(2,1)S(1)}, bf16[1,32,512]{2,1,0:T(8,128)(2,1)S(1)}, u32[]{:S(2)}, u32[]{:S(2)}) collective-permute-start(bf16[1,32,512]{2,1,0:T(8,128)(2,1)S(1)} %collective-permute-done.7), channel_id=1, source_target_pairs={{0,28},{4,0},{8,4},{12,8},{16,12},{20,16},{24,20},{28,24},{1,29},{... | collective-permute-start | bytes 98312 | tf_op jit(solution)/shard_map/ppermute | solution.py:16
  137.6 6.6 %collective-permute-start.9 = (bf16[1,32,512]{2,1,0:T(8,128)(2,1)S(1)}, bf16[1,32,512]{2,1,0:T(8,128)(2,1)S(1)}, u32[]{:S(2)}, u32[]{:S(2)}) collective-permute-start(bf16[1,32,512]{2,1,0:T(8,128)(2,1)S(1)} %collective-permute-done.8), channel_id=1, source_target_pairs={{0,28},{4,0},{8,4},{12,8},{16,12},{20,16},{24,20},{28,24},{1,29},{... | collective-permute-start | bytes 98312 | tf_op jit(solution)/shard_map/ppermute | solution.py:16
  144.2 6.6 %collective-permute-start.10 = (bf16[1,32,512]{2,1,0:T(8,128)(2,1)S(1)}, bf16[1,32,512]{2,1,0:T(8,128)(2,1)S(1)}, u32[]{:S(2)}, u32[]{:S(2)}) collective-permute-start(bf16[1,32,512]{2,1,0:T(8,128)(2,1)S(1)} %collective-permute-done.9), channel_id=1, source_target_pairs={{0,28},{4,0},{8,4},{12,8},{16,12},{20,16},{24,20},{28,24},{1,29},{... | collective-permute-start | bytes 98312 | tf_op jit(solution)/shard_map/ppermute | solution.py:16
  150.8 6.6 %collective-permute-start.11 = (bf16[1,32,512]{2,1,0:T(8,128)(2,1)S(1)}, bf16[1,32,512]{2,1,0:T(8,128)(2,1)S(1)}, u32[]{:S(2)}, u32[]{:S(2)}) collective-permute-start(bf16[1,32,512]{2,1,0:T(8,128)(2,1)S(1)} %collective-permute-done.10), channel_id=1, source_target_pairs={{0,28},{4,0},{8,4},{12,8},{16,12},{20,16},{24,20},{28,24},{1,29},{... | collective-permute-start | bytes 98312 | tf_op jit(solution)/shard_map/ppermute | solution.py:16
  157.4 6.7 %collective-permute-start.12 = (bf16[1,32,512]{2,1,0:T(8,128)(2,1)S(1)}, bf16[1,32,512]{2,1,0:T(8,128)(2,1)S(1)}, u32[]{:S(2)}, u32[]{:S(2)}) collective-permute-start(bf16[1,32,512]{2,1,0:T(8,128)(2,1)S(1)} %collective-permute-done.11), channel_id=1, source_target_pairs={{0,28},{4,0},{8,4},{12,8},{16,12},{20,16},{24,20},{28,24},{1,29},{... | collective-permute-start | bytes 98312 | tf_op jit(solution)/shard_map/ppermute | solution.py:16
  164.2 6.6 %collective-permute-start.13 = (bf16[1,32,512]{2,1,0:T(8,128)(2,1)S(1)}, bf16[1,32,512]{2,1,0:T(8,128)(2,1)S(1)}, u32[]{:S(2)}, u32[]{:S(2)}) collective-permute-start(bf16[1,32,512]{2,1,0:T(8,128)(2,1)S(1)} %collective-permute-done.12), channel_id=1, source_target_pairs={{0,28},{4,0},{8,4},{12,8},{16,12},{20,16},{24,20},{28,24},{1,29},{... | collective-permute-start | bytes 98312 | tf_op jit(solution)/shard_map/ppermute | solution.py:16
  180.2 8.6 %copy-start.1 = (bf16[1,2048,512]{2,1,0:T(8,128)(2,1)S(1)}, bf16[1,2048,512]{2,1,0:T(8,128)(2,1)}, u32[]{:S(2)}) copy-start(bf16[1,2048,512]{2,1,0:T(8,128)(2,1)} %get-tuple-element.895) | copy-start | bytes 6291460 | tf_op jit(solution)/shard_map/while
  189.4 8.6 %copy-start.1 = (bf16[1,2048,512]{2,1,0:T(8,128)(2,1)S(1)}, bf16[1,2048,512]{2,1,0:T(8,128)(2,1)}, u32[]{:S(2)}) copy-start(bf16[1,2048,512]{2,1,0:T(8,128)(2,1)} %get-tuple-element.895) | copy-start | bytes 6291460 | tf_op jit(solution)/shard_map/while
  198.6 8.6 %copy-start.1 = (bf16[1,2048,512]{2,1,0:T(8,128)(2,1)S(1)}, bf16[1,2048,512]{2,1,0:T(8,128)(2,1)}, u32[]{:S(2)}) copy-start(bf16[1,2048,512]{2,1,0:T(8,128)(2,1)} %get-tuple-element.895) | copy-start | bytes 6291460 | tf_op jit(solution)/shard_map/while
  207.9 8.6 %copy-start.1 = (bf16[1,2048,512]{2,1,0:T(8,128)(2,1)S(1)}, bf16[1,2048,512]{2,1,0:T(8,128)(2,1)}, u32[]{:S(2)}) copy-start(bf16[1,2048,512]{2,1,0:T(8,128)(2,1)} %get-tuple-element.895) | copy-start | bytes 6291460 | tf_op jit(solution)/shard_map/while
  217.1 8.6 %copy-start.1 = (bf16[1,2048,512]{2,1,0:T(8,128)(2,1)S(1)}, bf16[1,2048,512]{2,1,0:T(8,128)(2,1)}, u32[]{:S(2)}) copy-start(bf16[1,2048,512]{2,1,0:T(8,128)(2,1)} %get-tuple-element.895) | copy-start | bytes 6291460 | tf_op jit(solution)/shard_map/while
  226.3 8.6 %copy-start.1 = (bf16[1,2048,512]{2,1,0:T(8,128)(2,1)S(1)}, bf16[1,2048,512]{2,1,0:T(8,128)(2,1)}, u32[]{:S(2)}) copy-start(bf16[1,2048,512]{2,1,0:T(8,128)(2,1)} %get-tuple-element.895) | copy-start | bytes 6291460 | tf_op jit(solution)/shard_map/while
  235.6 8.6 %copy-start.1 = (bf16[1,2048,512]{2,1,0:T(8,128)(2,1)S(1)}, bf16[1,2048,512]{2,1,0:T(8,128)(2,1)}, u32[]{:S(2)}) copy-start(bf16[1,2048,512]{2,1,0:T(8,128)(2,1)} %get-tuple-element.895) | copy-start | bytes 6291460 | tf_op jit(solution)/shard_map/while
  (15 other events, 120.4 us)
